TPU v7x, 32 devices: a whole 2x2x4 slice. The times are simulated.
32 devices in a mesh: shift: 1, blk: 16 (over z, y, x), depth: 2 (over core).
Axes of the slice: x: 2, y: 2, z: 4, core: 2. Of those that a mesh axis runs over, the one named last changes fastest.
Arguments:
- density: bfloat16 [32, 32, 128, 128], P(('shift', 'blk')), may hold values from -1.1953125 to 1.1953125
- product_tasks: int32 [3, 16, 4, 128], P(None, ('shift', 'blk')), may hold values from 0 to 64, as said below
Outputs:
- square_blocks: bfloat16 [32, 32, 128, 128], P(('shift', 'blk'), 'depth')
Inputs may be any that keep to these rules, and one draw needn't show every extreme that they name: `product_tasks`: for each panel r and offset t the first tasks are exactly the triples in which slot a of panel r holds block (i, j) of P with block row j in panel (r + t) mod 16, slot b of that panel holds block (j, k), and c is the slot of block (i, k) in block row i, where P's block pattern stores 32 distinct block columns in each block row, its own among them; each triple once; the rest are (0, 0, 64). Some panel and offset has exactly 128 triples.
All inputs are finite; a program needn't handle non-finite values.
Results may differ from a plain program's by a relative error of at most 0.001.
Values may be sent and summed in bfloat16 or wider, within the bound.
A program may use at most 64 MiB of HBM per device.

v0:
```python
import jax
import jax.numpy as jnp
from jax import lax
from jax.sharding import PartitionSpec as P


def shifted(block, axis, distance):
    devices = range(lax.axis_size(axis))
    route = [((i - distance) % len(devices), i) for i in devices]
    return lax.ppermute(block, axis, route)


def multiply_step(total, mine, panel, tasks_now):
    count = tasks_now.shape[1]
    groups = 2
    grouped = tasks_now.reshape(3, groups, count // groups).transpose(1, 0, 2)
    segments = total.shape[0]

    def add_group(running, piece):
        first = jnp.take(mine, piece[0], axis=0)
        second = jnp.take(panel, piece[1], axis=0)
        products = jnp.einsum("nij,njk->nik", first, second, preferred_element_type=jnp.float32)
        return (running + jax.ops.segment_sum(products, piece[2], num_segments=segments), None)

    total, _ = lax.scan(add_group, total, grouped)
    return total


def body(density, product_tasks):
    rows, slots, size = (density.shape[0], density.shape[1], density.shape[2])
    mine = density.reshape(rows * slots, size, size)
    tasks_here = product_tasks[:, 0]
    window = tasks_here.shape[1]
    layers = lax.axis_size("depth")
    steps = window // layers
    layer = lax.axis_index("depth")
    total = jnp.zeros((rows * slots + 1, size, size), jnp.float32)
    distant = shifted(mine, "blk", -steps)
    panel = jnp.where(layer == 0, mine, distant)
    for step in range(steps):
        if step > 0:
            panel = shifted(panel, "blk", -1)
        offset = layer * steps + step
        tasks_now = lax.dynamic_index_in_dim(tasks_here, offset, 1, keepdims=False)
        total = multiply_step(total, mine, panel, tasks_now)
    partial_value = total[: rows * slots].reshape(rows, slots, size, size)
    summed = lax.psum_scatter(partial_value, "depth", scatter_dimension=1, tiled=True)
    return summed.astype(jnp.bfloat16)


def solution(mesh):
    placed = (P(("shift", "blk"), None, None, None), P(None, ("shift", "blk"), None, None))
    return jax.shard_map(
        body,
        mesh=mesh,
        in_specs=placed,
        out_specs=P(("shift", "blk"), "depth", None, None),
        check_vma=False,
    )
```

profile of v0, /device:TPU:0, one launch (start us, length us, event | category | flops | bytes accessed | tf_op | source)
XLA Modules:
  0.0 193.6 jit_solution(10912609643039239369)
XLA Ops:
  6.5 6.0 %collective-permute-start = (bf16[64,128,128]{2,1,0:T(8,128)(2,1)}, bf16[64,128,128]{2,1,0:T(8,128)(2,1)S(1)}, u32[]{:S(2)}, u32[]{:S(2)}) collective-permute-start(bf16[64,128,128]{2,1,0:T(8,128)(2,1)} %bitcast.58), channel_id=1, source_target_pairs={{4,0},{6,2},{8,4},{10,6},{12,8},{14,10},{16,12},{18,14},{20,16},{2... | collective-permute-start | bytes 6291464 | tf_op jit(solution)/shard_map/ppermute | solution.py:10
  12.6 45.2 %collective-permute-done = bf16[64,128,128]{2,1,0:T(8,128)(2,1)S(1)} collective-permute-done((bf16[64,128,128]{2,1,0:T(8,128)(2,1)}, bf16[64,128,128]{2,1,0:T(8,128)(2,1)S(1)}, u32[]{:S(2)}, u32[]{:S(2)}) %collective-permute-start) | collective-permute-done | bytes 2097184 | tf_op jit(solution)/shard_map/ppermute | solution.py:10
  57.8 3.1 %broadcast_select_fusion = bf16[64,128,128]{2,1,0:T(8,128)(2,1)} fusion(bf16[64,128,128]{2,1,0:T(8,128)(2,1)S(1)} %collective-permute-done, pred[]{:T(512)S(6)} %eq.3, bf16[2,32,128,128]{3,2,1,0:T(8,128)(2,1)} %param.8), kind=kLoop, calls=%fused_computation.46 | loop fusion | flops 1048576 | bytes 6291457 | tf_op jit(solution)/shard_map/jit(_where)/select_n | solution.py:39
  60.9 6.0 %collective-permute-start.1 = (bf16[64,128,128]{2,1,0:T(8,128)(2,1)}, bf16[64,128,128]{2,1,0:T(8,128)(2,1)}, u32[]{:S(2)}, u32[]{:S(2)}) collective-permute-start(bf16[64,128,128]{2,1,0:T(8,128)(2,1)} %broadcast_select_fusion), channel_id=1, source_target_pairs={{2,0},{4,2},{6,4},{8,6},{10,8},{12,10},{14,12},{16,14},{18,16},{20... | collective-permute-start | bytes 6291464 | tf_op jit(solution)/shard_map/ppermute | solution.py:10
  67.1 2.5 %broadcast.8 = f32[65,128,128]{2,1,0:T(8,128)} broadcast(f32[]{:T(128)} %constant.42.clone.1), dimensions={} | broadcast | bytes 4259844 | tf_op jit(solution)/shard_map/broadcast.5
  69.6 49.2 %while.20 = (s32[]{:T(128)}, f32[65,128,128]{2,1,0:T(8,128)}, s32[2,3,64]{2,0,1:T(2,128)S(1)}, bf16[64,128,128]{2,1,0:T(8,128)(2,1)S(1)}, bf16[64,128,128]{2,1,0...) while((s32[]{:T(128)}, f32[65,128,128]{2,1,0:T(8,128)}, s32[2,3,64]{2,0,1:T(2,128)S(1)}, ...), condition=%wide.region_2.4_spmd, body=%wide.region_0.3_spmd.sunk | while | flops 271584000 | bytes 29371524 | solution.py:25
  69.6 3.7 %gather_fusion = bf16[64,128,128]{2,1,0:T(8,128)(2,1)} fusion(bf16[64,128,128]{2,1,0:T(8,128)(2,1)} %get-tuple-element.228, s32[1024]{0:T(1024)S(1)} %get-tuple-element.191), kind=kCustom, calls=%fused_computation.1.clone.clone.1 | custom fusion | bytes 4194560 | tf_op jit(solution)/shard_map/while/body/eval_jaxpr/jit(_take)/gather | solution.py:21
  75.5 5.0 %fusion.31 = f32[64,128,128]{2,1,0:T(8,128)} fusion(bf16[64,128,128]{2,1,0:T(8,128)(2,1)} %gather_fusion, bf16[64,128,128]{2,1,0:T(8,128)(2,1)} %gather_fusion.1, pred[64]{0:T(512)(128)(4,1)S(1)} %get-tuple-element.193, pred[64]{0:T(512)(128)(4,1)S(1)} %get-tuple-element.194), kind=kOutput, calls=%fused_computation.6.clone.1 | convolution fusion | flops 270532608 | bytes 8388736 | tf_op jit(solution)/shard_map/while/body/eval_jaxpr/nij,njk->nik/dot_general | solution.py:22
  80.5 13.7 %scatter_fusion = f32[65,128,128]{2,1,0:T(8,128)} fusion(f32[65,128,128]{2,1,0:T(8,128)} %get-tuple-element.216, s32[64]{0:T(128)S(1)} %fusion.30, f32[64,128,128]{2,1,0:T(8,128)} %fusion.31), kind=kCustom, calls=%fused_computation.4.clone.1 | custom fusion | flops 1048576 | bytes 12583168 | tf_op jit(solution)/shard_map/while/body/eval_jaxpr/scatter-add | solution.py:23
  94.2 3.7 %gather_fusion = bf16[64,128,128]{2,1,0:T(8,128)(2,1)} fusion(bf16[64,128,128]{2,1,0:T(8,128)(2,1)} %get-tuple-element.228, s32[1024]{0:T(1024)S(1)} %get-tuple-element.191), kind=kCustom, calls=%fused_computation.1.clone.clone.1 | custom fusion | bytes 4194560 | tf_op jit(solution)/shard_map/while/body/eval_jaxpr/jit(_take)/gather | solution.py:21
  100.1 5.0 %fusion.31 = f32[64,128,128]{2,1,0:T(8,128)} fusion(bf16[64,128,128]{2,1,0:T(8,128)(2,1)} %gather_fusion, bf16[64,128,128]{2,1,0:T(8,128)(2,1)} %gather_fusion.1, pred[64]{0:T(512)(128)(4,1)S(1)} %get-tuple-element.193, pred[64]{0:T(512)(128)(4,1)S(1)} %get-tuple-element.194), kind=kOutput, calls=%fused_computation.6.clone.1 | convolution fusion | flops 270532608 | bytes 8388736 | tf_op jit(solution)/shard_map/while/body/eval_jaxpr/nij,njk->nik/dot_general | solution.py:22
  105.1 13.7 %scatter_fusion = f32[65,128,128]{2,1,0:T(8,128)} fusion(f32[65,128,128]{2,1,0:T(8,128)} %get-tuple-element.216, s32[64]{0:T(128)S(1)} %fusion.30, f32[64,128,128]{2,1,0:T(8,128)} %fusion.31), kind=kCustom, calls=%fused_computation.4.clone.1 | custom fusion | flops 1048576 | bytes 12583168 | tf_op jit(solution)/shard_map/while/body/eval_jaxpr/scatter-add | solution.py:23
  118.8 49.0 %while.21 = (s32[]{:T(128)}, f32[65,128,128]{2,1,0:T(8,128)}, s32[2,3,64]{2,0,1:T(2,128)S(1)}, bf16[64,128,128]{2,1,0:T(8,128)(2,1)S(1)}, bf16[64,128,128]{2,1,0...) while((s32[]{:T(128)}, f32[65,128,128]{2,1,0:T(8,128)}, s32[2,3,64]{2,0,1:T(2,128)S(1)}, ...), condition=%wide.region_5.7_spmd, body=%wide.region_3.6_spmd.sunk | while | flops 271584000 | bytes 29371524 | solution.py:25
  118.8 3.7 %gather_fusion.2 = bf16[64,128,128]{2,1,0:T(8,128)(2,1)} fusion(bf16[64,128,128]{2,1,0:T(8,128)(2,1)} %get-tuple-element.255, s32[1024]{0:T(1024)S(1)} %get-tuple-element.202), kind=kCustom, calls=%fused_computation.3.clone.clone.1 | custom fusion | bytes 4194560 | tf_op jit(solution)/shard_map/while/body/eval_jaxpr/jit(_take)/gather | solution.py:21
  122.5 2.1 %gather_fusion.3 = bf16[64,128,128]{2,1,0:T(8,128)(2,1)} fusion(bf16[64,128,128]{2,1,0:T(8,128)(2,1)S(1)} %get-tuple-element.254, s32[1024]{0:T(1024)S(1)} %get-tuple-element.203), kind=kCustom, calls=%fused_computation.2.clone.clone.1 | custom fusion | bytes 4194560 | tf_op jit(solution)/shard_map/while/body/eval_jaxpr/jit(_take)/gather | solution.py:20
  124.7 5.0 %fusion.35 = f32[64,128,128]{2,1,0:T(8,128)} fusion(bf16[64,128,128]{2,1,0:T(8,128)(2,1)} %gather_fusion.2, bf16[64,128,128]{2,1,0:T(8,128)(2,1)} %gather_fusion.3, pred[64]{0:T(512)(128)(4,1)S(1)} %get-tuple-element.204, pred[64]{0:T(512)(128)(4,1)S(1)} %get-tuple-element.205), kind=kOutput, calls=%fused_computation.25.clone.1 | convolution fusion | flops 270532608 | bytes 8388736 | tf_op jit(solution)/shard_map/while/body/eval_jaxpr/nij,njk->nik/dot_general | solution.py:22
  129.7 13.6 %scatter_fusion.1 = f32[65,128,128]{2,1,0:T(8,128)} fusion(f32[65,128,128]{2,1,0:T(8,128)} %get-tuple-element.243, s32[64]{0:T(128)S(1)} %fusion.34, f32[64,128,128]{2,1,0:T(8,128)} %fusion.35), kind=kCustom, calls=%fused_computation.5.clone.1 | custom fusion | flops 1048576 | bytes 12583168 | tf_op jit(solution)/shard_map/while/body/eval_jaxpr/scatter-add | solution.py:23
  143.3 3.7 %gather_fusion.2 = bf16[64,128,128]{2,1,0:T(8,128)(2,1)} fusion(bf16[64,128,128]{2,1,0:T(8,128)(2,1)} %get-tuple-element.255, s32[1024]{0:T(1024)S(1)} %get-tuple-element.202), kind=kCustom, calls=%fused_computation.3.clone.clone.1 | custom fusion | bytes 4194560 | tf_op jit(solution)/shard_map/while/body/eval_jaxpr/jit(_take)/gather | solution.py:21
  147.0 2.1 %gather_fusion.3 = bf16[64,128,128]{2,1,0:T(8,128)(2,1)} fusion(bf16[64,128,128]{2,1,0:T(8,128)(2,1)S(1)} %get-tuple-element.254, s32[1024]{0:T(1024)S(1)} %get-tuple-element.203), kind=kCustom, calls=%fused_computation.2.clone.clone.1 | custom fusion | bytes 4194560 | tf_op jit(solution)/shard_map/while/body/eval_jaxpr/jit(_take)/gather | solution.py:20
  149.2 5.0 %fusion.35 = f32[64,128,128]{2,1,0:T(8,128)} fusion(bf16[64,128,128]{2,1,0:T(8,128)(2,1)} %gather_fusion.2, bf16[64,128,128]{2,1,0:T(8,128)(2,1)} %gather_fusion.3, pred[64]{0:T(512)(128)(4,1)S(1)} %get-tuple-element.204, pred[64]{0:T(512)(128)(4,1)S(1)} %get-tuple-element.205), kind=kOutput, calls=%fused_computation.25.clone.1 | convolution fusion | flops 270532608 | bytes 8388736 | tf_op jit(solution)/shard_map/while/body/eval_jaxpr/nij,njk->nik/dot_general | solution.py:22
  154.2 13.6 %scatter_fusion.1 = f32[65,128,128]{2,1,0:T(8,128)} fusion(f32[65,128,128]{2,1,0:T(8,128)} %get-tuple-element.243, s32[64]{0:T(128)S(1)} %fusion.34, f32[64,128,128]{2,1,0:T(8,128)} %fusion.35), kind=kCustom, calls=%fused_computation.5.clone.1 | custom fusion | flops 1048576 | bytes 12583168 | tf_op jit(solution)/shard_map/while/body/eval_jaxpr/scatter-add | solution.py:23
  167.8 2.5 %slice.27 = f32[64,128,128]{2,1,0:T(8,128)S(1)} slice(f32[65,128,128]{2,1,0:T(8,128)} %get-tuple-element.61), slice={[0:64], [0:128], [0:128]} | slice | bytes 8388608 | tf_op jit(solution)/shard_map/slice | solution.py:46
  170.8 4.4 %copy.22 = f32[4,8,256,128]{3,1,2,0:T(8,128)} copy(f32[4,8,256,128]{3,2,1,0:T(8,128)S(1)} %bitcast.62) | data formatting | bytes 8388608
  175.1 8.5 %reduce-scatter.5.cloned.1.call-done = f32[16,32768]{1,0:T(8,128)} async-done(((f32[32,32768]{1,0:T(8,128)}), f32[16,32768]{1,0:T(8,128)}) %reduce-scatter.5.cloned.1.call-update) | async-done | bytes 2097168
  (27 shorter events, 8.1 us)
Async XLA Ops:
  6.5 177.1 %reduce-scatter.5.cloned.1.call-start = ((), (), s32[]{:S(2)}) async-start(), calls=%async_computation.1 | async-start | bytes 6291456
  6.5 51.2 %collective-permute-start = (bf16[64,128,128]{2,1,0:T(8,128)(2,1)}, bf16[64,128,128]{2,1,0:T(8,128)(2,1)S(1)}, u32[]{:S(2)}, u32[]{:S(2)}) collective-permute-start(bf16[64,128,128]{2,1,0:T(8,128)(2,1)} %bitcast.58), channel_id=1, source_target_pairs={{4,0},{6,2},{8,4},{10,6},{12,8},{14,10},{16,12},{18,14},{20,16},{2... | collective-permute-start | bytes 6291464 | tf_op jit(solution)/shard_map/ppermute | solution.py:10
  12.6 54.3 %copy-start.1 = (s32[3,1,4,128]{3,2,1,0:T(4,128)S(1)}, s32[3,1,4,128]{3,2,1,0:T(4,128)}, u32[]{:S(2)}) copy-start(s32[3,1,4,128]{3,2,1,0:T(4,128)} %param.9) | copy-start | bytes 18436
  60.9 57.9 %collective-permute-start.1 = (bf16[64,128,128]{2,1,0:T(8,128)(2,1)}, bf16[64,128,128]{2,1,0:T(8,128)(2,1)}, u32[]{:S(2)}, u32[]{:S(2)}) collective-permute-start(bf16[64,128,128]{2,1,0:T(8,128)(2,1)} %broadcast_select_fusion), channel_id=1, source_target_pairs={{2,0},{4,2},{6,4},{8,6},{10,8},{12,10},{14,12},{16,14},{18,16},{20... | collective-permute-start | bytes 6291464 | tf_op jit(solution)/shard_map/ppermute | solution.py:10
  67.1 2.5 %copy-start = (bf16[2,32,128,128]{3,2,1,0:T(8,128)(2,1)S(1)}, bf16[2,32,128,128]{3,2,1,0:T(8,128)(2,1)}, u32[]{:S(2)}) copy-start(bf16[2,32,128,128]{3,2,1,0:T(8,128)(2,1)} %param.8) | copy-start | bytes 6291460
Sparse Core Ops, SparseCore 0:
  175.3 8.3 reduce-scatter.4
where the time goes:
time: 194 us
  other arithmetic  57.9 us (30%)
  waiting for transfers between devices  53.8 us (28%)
  local copies, waits for them, and re-layouts  36.5 us (19%)
  matrix products  20 us (10%)
  between operations  13.4 us (7%)
  starting transfers between devices  12 us (6%)
    scatter-add x4, other arithmetic, add_group(): jax.ops.segment_sum(products, piece[2], num_segments=segments)  54.7 us
    ppermute x2, waiting for transfers between devices, shifted(): return lax.ppermute(block, axis, route)  45.2 us
    dot_general x4, matrix products, add_group(): jnp.einsum('nij,njk->nik', first, second, preferred_element_type=jnp.floa...  20 us
    gather x4, local copies, waits for them, and re-layouts, add_group(): second = jnp.take(panel, piece[1], axis=0)  14.9 us
    ppermute x2, starting transfers between devices, shifted(): return lax.ppermute(block, axis, route)  12 us
    unnamed x2, waiting for transfers between devices  8.55 us
    gather x4, local copies, waits for them, and re-layouts, add_group(): first = jnp.take(mine, piece[0], axis=0)  8.53 us
    unnamed x8, local copies, waits for them, and re-layouts  7.94 us
  transfers between devices with their start and end apart: 3, of which 2 were waited for; matrix products, arithmetic and copies ran while one was open for 27% of the time, Pallas kernels for 0%

commit v1 on v0

v1 whole, which is shorter than its diff:
```python
import functools

import jax
import jax.numpy as jnp
from jax import lax
from jax.experimental import pallas as pl
from jax.experimental.pallas import tpu as pltpu
from jax.sharding import PartitionSpec as P

MESH = pl.DeviceIdType.MESH
GROUP = 4
PASS = 0

OWN = {
    (0, 0): [(-1, 0, PASS)],
    (0, 1): [(-1, 0, PASS)],
    (1, 0): [(0, 0, 1), (-1, 1, PASS)],
    (1, 1): [(0, 0, 1), (-1, 1, PASS)],
    (2, 0): [(0, 0, 2), (-1, 2, PASS)],
    (2, 1): [(0, 0, 2), (0, 3, PASS)],
    (3, 0): [(0, 2, 1), (0, 1, 2)],
    (3, 1): [(0, 2, 1), (0, 1, 2)],
}
FIRST = {
    (0, 0): [(PASS, [(0, 1, 3), (0, 2, 2)]), (1, []), (2, [(0, 1, 1)])],
    (0, 1): [(PASS, [(0, 1, 3), (0, 2, 2)]), (1, [(0, 2, PASS)]), (2, [])],
    (1, 0): [(PASS, [(0, 3, 2)]), (2, []), (3, [(0, 3, 1)])],
    (1, 1): [(PASS, [(0, 3, 2)]), (2, [(0, 0, 3)]), (3, [])],
    (2, 0): [(PASS, [(0, 3, 3)]), (1, [(0, 0, 3)]), (2, [])],
    (2, 1): [(1, []), (2, [(0, 3, 1)]), (PASS, [(-1, 2, 3)])],
    (3, 0): [(2, [(0, 2, 3)])],
    (3, 1): [(PASS, [(-1, 3, 3), (0, 1, 1)]), (2, [])],
}
LAST = {
    (0, 0): [3],
    (0, 1): [3],
    (1, 0): [1],
    (1, 1): [1],
    (2, 0): [3],
    (2, 1): [3],
    (3, 0): [1, 3],
    (3, 1): [1, 3],
}


def kernel(n, density, tasks, out, *scratch):
    rows, slots, size = density.shape[0], density.shape[1], density.shape[2]
    window, count = tasks.shape[2], tasks.shape[3]
    win = scratch[:window]
    relay, lines, table, spots, send, got, give, take, local = scratch[window:]
    stored = rows * slots
    half = slots
    chunks = got.shape[1]
    part = half // chunks
    me = lax.axis_index("blk")
    h = lax.axis_index("depth")
    q = me % GROUP
    base = me - q

    def place(step, spot):
        return (base + step * GROUP + n + spot) % n

    def there(step, spot):
        return {"blk": place(step, spot)}

    partner = {"depth": 1 - h}
    barrier = pltpu.get_barrier_semaphore()
    greeted = [
        partner,
        {"blk": base + (q ^ 1)},
        {"blk": base + (q ^ 2)},
        {"blk": (me + GROUP) % n},
        {"blk": (me + n - GROUP) % n},
    ]
    for other in greeted:
        pl.semaphore_signal(barrier, inc=1, device_id=other, device_id_type=MESH)
    pl.semaphore_wait(barrier, len(greeted))

    def held(buffer, side, k, length):
        if buffer == PASS:
            return relay.at[pl.ds(k * part, length)]
        return win[buffer].at[pl.ds(side * half + k * part, length)]

    def remote(source, target, lane, k, length=part):
        step, spot, buffer = target
        return pltpu.make_async_remote_copy(
            src_ref=source,
            dst_ref=held(buffer, h, k, length),
            send_sem=send.at[lane],
            recv_sem=got.at[buffer, k],
            device_id=there(step, spot),
            device_id_type=MESH,
        )

    def passed(buffer, side, k, length=part):
        return pltpu.make_async_remote_copy(
            src_ref=held(buffer, side, k, length),
            dst_ref=held(buffer, side, k, length),
            send_sem=give.at[buffer],
            recv_sem=take.at[buffer],
            device_id=partner,
            device_id_type=MESH,
        )

    def roles(emit):
        for role in OWN:

            @pl.when(jnp.logical_and(q == role[0], h == role[1]))
            def _(role=role):
                emit(role)

    def emit_own(role):
        side = role[1]

        def push(k, _):
            source = density.at[side, pl.ds(k * part, part)]
            for lane, target in enumerate(OWN[role]):
                remote(source, target, lane, k).start()
            return 0

        lax.fori_loop(0, chunks, push, 0)

    roles(emit_own)

    mine = [
        pltpu.make_async_copy(density.at[r], win[0].at[pl.ds(r * slots, slots)], local.at[r])
        for r in range(rows)
    ]
    for copy in mine:
        copy.start()
    for t in range(window):
        win[t][stored] = jnp.zeros((size, size), density.dtype)

    mine_slots = out.shape[1]
    entries = rows * mine_slots * rows
    entry = lax.broadcasted_iota(jnp.int32, (entries, count), 0)
    column = lax.broadcasted_iota(jnp.int32, (entries, count), 1)
    entry_row = entry // (mine_slots * rows)
    entry_slot = entry // rows % mine_slots
    entry_inner = entry % rows
    wanted = entry_row * slots + h * mine_slots + entry_slot
    found = jnp.zeros((entries, count), jnp.int32)
    for t in range(window):
        first = jnp.broadcast_to(tasks[0, 0, t : t + 1, :], (entries, count))
        second = jnp.broadcast_to(tasks[1, 0, t : t + 1, :], (entries, count))
        result = jnp.broadcast_to(tasks[2, 0, t : t + 1, :], (entries, count))
        inner_ok = second // slots == entry_inner
        hit = jnp.logical_and(inner_ok, result == wanted)
        spot = jnp.max(jnp.where(hit, second, -1), axis=1, keepdims=True)
        spot = jnp.where(spot < 0, stored, spot)
        hit_row = jnp.logical_and(inner_ok, result // slots == entry_row)
        line = jnp.max(jnp.where(hit_row, first, 0), axis=1, keepdims=True)
        found = jnp.where(column == t, spot, found)
        found = jnp.where(column == window + t, line, found)
    table[...] = found
    fetch = pltpu.make_async_copy(table, spots, local.at[rows])
    fetch.start()
    fetch.wait()
    for copy in mine:
        copy.wait()

    for r in range(rows):
        for t in range(window):
            for j in range(rows):
                spot = spots[r * mine_slots * rows + j, window + t]
                at = (t * rows + j) * size
                lines[r, :, at : at + size] = win[0][spot]

    def emit_flow(role):
        side = role[1]

        def arrive(k, buffer, onward, lane):
            remote(held(buffer, side, k, part), (0, role[0], buffer), 0, k).wait_recv()
            for target in onward:
                remote(held(buffer, side, k, part), target, lane, k).start()
                lane += 1
            if buffer != PASS:
                passed(buffer, side, k).start()
            return lane

        def early(k, _):
            lane = len(OWN[role])
            for buffer, onward in FIRST[role]:
                lane = arrive(k, buffer, onward, lane)
            return 0

        def late(k, _):
            for buffer in LAST[role]:
                arrive(k, buffer, [], 0)
            return 0

        lax.fori_loop(0, chunks, early, 0)
        lax.fori_loop(0, chunks, late, 0)
        sent = len(OWN[role]) + sum(len(onward) for _, onward in FIRST[role])
        for lane in range(sent):
            remote(held(PASS, side, 0, half), (0, role[0], PASS), lane, 0, half).wait_send()

    roles(emit_flow)
    for t in range(1, window):
        passed(t, 1 - h, 0, half).wait_recv()
        passed(t, h, 0, half).wait_send()

    pair = 2
    for r in range(rows):

        def multiply(m, _, r=r):
            columns = []
            for s in range(pair):
                at = (r * mine_slots + m * pair + s) * rows
                blocks = [win[t][spots[at + j, t]] for t in range(window) for j in range(rows)]
                columns.append(jnp.concatenate(blocks, axis=0))
            right = jnp.concatenate(columns, axis=1)
            value = jnp.dot(lines[r], right, preferred_element_type=jnp.float32)
            for s in range(pair):
                out[r, m * pair + s] = value[:, s * size : (s + 1) * size].astype(out.dtype)
            return 0

        lax.fori_loop(0, mine_slots // pair, multiply, 0)


def solution(mesh):
    n = mesh.shape["blk"]
    layers = mesh.shape["depth"]

    def body(density, product_tasks):
        rows, slots, size = density.shape[0], density.shape[1], density.shape[2]
        window, count = product_tasks.shape[2], product_tasks.shape[3]
        stored = rows * slots
        mine_slots = slots // layers
        entries = rows * mine_slots * rows
        chunks = 8
        lanes = max(len(OWN[r]) + sum(len(o) for _, o in FIRST[r]) for r in OWN)
        return pl.pallas_call(
            functools.partial(kernel, n),
            out_shape=jax.ShapeDtypeStruct((rows, mine_slots, size, size), density.dtype),
            in_specs=[
                pl.BlockSpec(memory_space=pl.ANY),
                pl.BlockSpec(memory_space=pltpu.VMEM),
            ],
            out_specs=pl.BlockSpec(memory_space=pltpu.VMEM),
            scratch_shapes=[
                *[pltpu.VMEM((stored + 1, size, size), density.dtype)] * window,
                pltpu.VMEM((slots, size, size), density.dtype),
                pltpu.VMEM((rows, size, window * rows * size), density.dtype),
                pltpu.VMEM((entries, count), jnp.int32),
                pltpu.SMEM((entries, count), jnp.int32),
                pltpu.SemaphoreType.DMA((lanes,)),
                pltpu.SemaphoreType.DMA((window, chunks)),
                pltpu.SemaphoreType.DMA((window,)),
                pltpu.SemaphoreType.DMA((window,)),
                pltpu.SemaphoreType.DMA((rows + 1,)),
            ],
            compiler_params=pltpu.CompilerParams(collective_id=0, has_side_effects=True),
        )(density, product_tasks)

    placed = (P(("shift", "blk"), None, None, None), P(None, ("shift", "blk"), None, None))
    return jax.shard_map(
        body,
        mesh=mesh,
        in_specs=placed,
        out_specs=P(("shift", "blk"), "depth", None, None),
        check_vma=False,
    )
```

time: 194 us -> 57.8 us (0.30)
  the two profiles are of different devices: /device:TPU:0 before, /device:TPU:29 now
where the time goes in v1:
time: 57.8 us; the launch traced here: 57.6 us
  Pallas kernels  55.3 us (96%)
  local copies, waits for them, and re-layouts  2.31 us (4%)
    pallas_call x1, Pallas kernels, body(): pl.pallas_call(functools.partial(kernel, n), out_shape=jax.ShapeDtypeStru...  55.3 us
    unnamed x1, local copies, waits for them, and re-layouts  2.31 us

profile of v1, /device:TPU:29, one launch (start us, length us, event | category | flops | bytes accessed | tf_op | source)
XLA Modules:
  0.0 57.6 jit_solution(5601046093030734990)
XLA Ops:
  0.0 55.3 %shard_map.28 = bf16[2,16,128,128]{3,2,1,0:T(8,128)(2,1)} custom-call(bf16[2,32,128,128]{3,2,1,0:T(8,128)(2,1)} %density.1, s32[3,1,4,128]{3,2,1,0:T(4,128)} %tasks.1), custom_call_target="tpu_custom_call" | custom-call | tf_op jit(solution)/shard_map/pallas_call | solution.py:233
  55.3 2.3 %copy.4 = bf16[2,16,128,128]{3,2,1,0:T(8,128)(2,1)} copy(bf16[2,16,128,128]{3,2,1,0:T(8,128)(2,1)} %shard_map.28) | data formatting | bytes 2097152

commit v2 on v1

v2 whole, which is shorter than its diff:
```python
import functools
import heapq

import jax
import jax.numpy as jnp
from jax import lax
from jax.experimental import pallas as pl
from jax.experimental.pallas import tpu as pltpu
from jax.sharding import PartitionSpec as P

MESH = pl.DeviceIdType.MESH
GROUP = 4

TREES = {
    (0, 0): [((0, 0), (0, 1)), ((0, 1), (-1, 1)), ((-1, 1), (-1, 3)), ((0, 0), (-1, 0)), ((-1, 0), (-1, 2))],
    (0, 1): [((0, 0), (0, 2)), ((0, 2), (-1, 2)), ((-1, 2), (-1, 3)), ((0, 0), (-1, 0)), ((-1, 0), (-1, 1))],
    (1, 0): [((0, 1), (0, 0)), ((0, 1), (0, 3)), ((0, 3), (-1, 3)), ((-1, 3), (-1, 2))],
    (1, 1): [((0, 1), (0, 0)), ((0, 1), (-1, 1)), ((0, 0), (0, 2)), ((0, 2), (-1, 2)), ((-1, 1), (-1, 3))],
    (2, 0): [((0, 2), (0, 0)), ((0, 2), (-1, 2)), ((0, 0), (0, 1)), ((-1, 2), (-1, 3))],
    (2, 1): [((0, 2), (0, 3)), ((0, 2), (0, 0)), ((0, 3), (0, 1)), ((0, 3), (-1, 3))],
    (3, 0): [((0, 3), (0, 2)), ((0, 3), (0, 1)), ((0, 2), (0, 0))],
    (3, 1): [((0, 3), (0, 1)), ((0, 3), (0, 2)), ((0, 1), (0, 0))],
}
LINK_TIME = 1.41 / 65536
HOP_TIME = 1.6
SLACK = 3.0


def buffers():
    found, used = {}, {}
    for (panel, tree), edges in TREES.items():
        for _, (step, spot) in edges:
            offset = panel - spot - GROUP * step
            if not 0 < offset < GROUP:
                offset = used.get((spot, tree), GROUP)
                used[spot, tree] = offset + 1
            found[panel, tree, (step, spot)] = offset
    return found, max(used.values())


def make_plan(chunks, chunk_bytes):
    filled, total = buffers()

    def hop(panel, tree, source, target):
        return (target[0] - source[0], target[1], filled[panel, tree, target])

    first = []
    for (panel, tree), edges in TREES.items():
        for source, target in edges:
            if source == (0, panel):
                leaf = all(after != target for after, _ in edges)
                first += [(leaf, k, panel, tree, source, target) for k in range(chunks)]
    first.sort(key=lambda item: item[:2])
    own, seen = {q: [] for q in range(GROUP)}, {q: [] for q in range(GROUP)}
    queue, free = [], {}
    for serial, (_, k, panel, tree, source, target) in enumerate(first):
        heapq.heappush(queue, (0.0, serial, panel, tree, k, source, target))
        own[panel].append((tree, k, hop(panel, tree, source, target)))
    serial = len(first)
    while queue:
        now, _, panel, tree, k, source, target = heapq.heappop(queue)
        link = (source[1], target[1], target[0] - source[0])
        free[link] = max(now, free.get(link, 0.0)) + chunk_bytes * LINK_TIME
        done = free[link] + HOP_TIME
        onward = []
        for after, further in TREES[panel, tree]:
            if after == target:
                heapq.heappush(queue, (done, serial, panel, tree, k, after, further))
                serial += 1
                onward.append(hop(panel, tree, after, further))
        seen[target[1]].append((done, filled[panel, tree, target], (tree, k, onward)))
    events, tails = {}, {}
    for spot, arrivals in seen.items():
        end = max(done for done, _, _ in arrivals)
        mixed, tails[spot] = list(arrivals), []
        for t in range(1, GROUP):
            ready = max(done for done, buffer, _ in arrivals if buffer == t) + SLACK
            if ready < end - SLACK:
                mixed.append((ready, t, None))
            else:
                tails[spot].append(t)
        events[spot] = sorted(mixed, key=lambda event: event[0])
    return own, events, tails, total


def kernel(n, own, events, tails, density, tasks_in, out, *scratch):
    rows, slots, size = density.shape[0], density.shape[1], density.shape[2]
    window, count = tasks_in.shape[2], tasks_in.shape[3]
    win = scratch[:window]
    relay, lines, total, tasks, table, spots, send, got, give, take, local = scratch[window:]
    stored = rows * slots
    half = slots
    trees, chunks = got.shape[1], got.shape[2]
    part = half // (trees * chunks)
    me = lax.axis_index("blk")
    h = lax.axis_index("depth")
    q = me % GROUP
    base = me - q

    def place(step, spot):
        return (base + step * GROUP + n + spot) % n

    def there(step, spot):
        return {"blk": place(step, spot)}

    partner = {"depth": 1 - h}
    barrier = pltpu.get_barrier_semaphore()
    greeted = [
        partner,
        {"blk": base + (q ^ 1)},
        {"blk": base + (q ^ 2)},
        {"blk": (me + GROUP) % n},
        {"blk": (me + n - GROUP) % n},
    ]
    for other in greeted:
        pl.semaphore_signal(barrier, inc=1, device_id=other, device_id_type=MESH)
    pl.semaphore_wait(barrier, len(greeted))

    def held(buffer, side, at, length):
        if buffer >= window:
            return relay.at[pl.ds((buffer - window) * half + at, length)]
        return win[buffer].at[pl.ds(side * half + at, length)]

    def start(source, tree, k, hop):
        step, spot, buffer = hop
        at = (tree * chunks + k) * part
        pltpu.make_async_remote_copy(
            src_ref=source,
            dst_ref=held(buffer, h, at, part),
            send_sem=send.at[0],
            recv_sem=got.at[buffer, tree, k],
            device_id=there(step, spot),
            device_id_type=MESH,
        ).start()

    def passed(buffer, side, at, length):
        return pltpu.make_async_remote_copy(
            src_ref=held(buffer, side, at, length),
            dst_ref=held(buffer, side, at, length),
            send_sem=give.at[buffer],
            recv_sem=take.at[buffer],
            device_id=partner,
            device_id_type=MESH,
        )

    def places(emit):
        for spot in range(GROUP):

            @pl.when(q == spot)
            def _(spot=spot):
                emit(spot)

    def emit_own(spot):
        for tree, k, hop in own[spot]:
            at = (tree * chunks + k) * part
            start(density.at[h, pl.ds(at, part)], tree, k, hop)

    places(emit_own)

    mine = [
        pltpu.make_async_copy(density.at[r], win[0].at[pl.ds(r * slots, slots)], local.at[r])
        for r in range(rows)
    ]
    listed = pltpu.make_async_copy(tasks_in, tasks, local.at[rows])
    listed.start()
    for copy in mine:
        copy.start()
    for t in range(window):
        win[t][stored] = jnp.zeros((size, size), density.dtype)

    listed.wait()
    mine_slots = out.shape[1]
    entries = rows * mine_slots * rows
    entry = lax.broadcasted_iota(jnp.int32, (entries, count), 0)
    column = lax.broadcasted_iota(jnp.int32, (entries, count), 1)
    entry_row = entry // (mine_slots * rows)
    entry_slot = entry // rows % mine_slots
    entry_inner = entry % rows
    wanted = entry_row * slots + h * mine_slots + entry_slot
    found = jnp.zeros((entries, count), jnp.int32)
    for t in range(window):
        first = jnp.broadcast_to(tasks[0, 0, t : t + 1, :], (entries, count))
        second = jnp.broadcast_to(tasks[1, 0, t : t + 1, :], (entries, count))
        result = jnp.broadcast_to(tasks[2, 0, t : t + 1, :], (entries, count))
        inner_ok = second // slots == entry_inner
        hit = jnp.logical_and(inner_ok, result == wanted)
        spot = jnp.max(jnp.where(hit, second, -1), axis=1, keepdims=True)
        spot = jnp.where(spot < 0, stored, spot)
        hit_row = jnp.logical_and(inner_ok, result // slots == entry_row)
        line = jnp.max(jnp.where(hit_row, first, 0), axis=1, keepdims=True)
        found = jnp.where(column == t, spot, found)
        found = jnp.where(column == window + t, line, found)
    table[...] = found
    fetch = pltpu.make_async_copy(table, spots, local.at[rows])
    fetch.start()
    fetch.wait()
    for copy in mine:
        copy.wait()

    for r in range(rows):
        for t in range(window):
            for j in range(rows):
                spot = spots[r * mine_slots * rows + j, window + t]
                at = (t * rows + j) * size
                lines[r, :, at : at + size] = win[0][spot]

    pair = 2

    def multiply(offsets, begin, end):
        for t in offsets:
            if t > 0:
                passed(t, 1 - h, 0, half).wait_recv()
                passed(t, h, 0, half).wait_send()
        width = rows * size
        for r in range(rows):

            def step(m, _, r=r):
                columns = []
                for s in range(pair):
                    at = (r * mine_slots + m * pair + s) * rows
                    blocks = [win[t][spots[at + j, t]] for t in offsets for j in range(rows)]
                    columns.append(jnp.concatenate(blocks, axis=0))
                right = jnp.concatenate(columns, axis=1)
                left = jnp.concatenate([lines[r, :, t * width : (t + 1) * width] for t in offsets], axis=1)
                value = jnp.dot(left, right, preferred_element_type=jnp.float32)
                if not begin:
                    value = value + total[r, m]
                if not end:
                    total[r, m] = value
                    return 0
                for s in range(pair):
                    out[r, m * pair + s] = value[:, s * size : (s + 1) * size].astype(out.dtype)
                return 0

            lax.fori_loop(0, mine_slots // pair, step, 0)

    def emit_flow(spot):
        sent = len(own[spot])
        for _, buffer, event in events[spot]:
            if event is None:
                multiply([buffer], False, False)
                continue
            tree, k, onward = event
            at = (tree * chunks + k) * part
            chunk = held(buffer, h, at, part)
            pltpu.make_async_copy(chunk, chunk, got.at[buffer, tree, k]).wait()
            for hop in onward:
                start(chunk, tree, k, hop)
            sent += len(onward)
            if buffer < window:
                passed(buffer, h, at, part).start()
        multiply(tails[spot], False, True)
        left = sent * part
        while left > 0:
            length = min(left, half)
            chunk = held(window, h, 0, length)
            pltpu.make_async_copy(chunk, chunk, send.at[0]).wait()
            left -= length

    multiply([0], True, False)
    places(emit_flow)


def solution(mesh):
    n = mesh.shape["blk"]
    layers = mesh.shape["depth"]

    def body(density, product_tasks):
        rows, slots, size = density.shape[0], density.shape[1], density.shape[2]
        window, count = product_tasks.shape[2], product_tasks.shape[3]
        stored = rows * slots
        mine_slots = slots // layers
        entries = rows * mine_slots * rows
        chunks = 8
        trees = 2
        chunk_bytes = slots // (trees * chunks) * size * size * density.dtype.itemsize
        own, events, tails, total = make_plan(chunks, chunk_bytes)
        return pl.pallas_call(
            functools.partial(kernel, n, own, events, tails),
            out_shape=jax.ShapeDtypeStruct((rows, mine_slots, size, size), density.dtype),
            in_specs=[
                pl.BlockSpec(memory_space=pltpu.HBM),
                pl.BlockSpec(memory_space=pltpu.HBM),
            ],
            out_specs=pl.BlockSpec(memory_space=pltpu.VMEM),
            scratch_shapes=[
                *[pltpu.VMEM((stored + 1, size, size), density.dtype)] * window,
                pltpu.VMEM(((total - window) * slots, size, size), density.dtype),
                pltpu.VMEM((rows, size, window * rows * size), density.dtype),
                pltpu.VMEM((rows, mine_slots // 2, size, 2 * size), jnp.float32),
                pltpu.VMEM(product_tasks.shape, jnp.int32),
                pltpu.VMEM((entries, count), jnp.int32),
                pltpu.SMEM((entries, count), jnp.int32),
                pltpu.SemaphoreType.DMA((1,)),
                pltpu.SemaphoreType.DMA((total, trees, chunks)),
                pltpu.SemaphoreType.DMA((window,)),
                pltpu.SemaphoreType.DMA((window,)),
                pltpu.SemaphoreType.DMA((rows + 1,)),
            ],
            compiler_params=pltpu.CompilerParams(collective_id=0, has_side_effects=True, vmem_limit_bytes=24 << 20),
        )(density, product_tasks)

    placed = (P(("shift", "blk"), None, None, None), P(None, ("shift", "blk"), None, None))
    return jax.shard_map(
        body,
        mesh=mesh,
        in_specs=placed,
        out_specs=P(("shift", "blk"), "depth", None, None),
        check_vma=False,
    )
```

time: 57.8 us -> 48.9 us (0.85)
  the two profiles are of different devices: /device:TPU:29 before, /device:TPU:0 now
where the time goes in v2:
time: 48.9 us; the launch traced here: 48.8 us
  Pallas kernels  45.5 us (93%)
  local copies, waits for them, and re-layouts  3.25 us (7%)
    pallas_call x1, Pallas kernels, body(): pl.pallas_call(functools.partial(kernel, n, own, events, tails), out_shap...  45.5 us
    unnamed x5, local copies, waits for them, and re-layouts  3.25 us

profile of v2, /device:TPU:0, one launch (start us, length us, event | category | flops | bytes accessed | tf_op | source)
XLA Modules:
  0.0 48.8 jit_solution(14449523163119292957)
XLA Ops:
  0.0 0.0 copy-start
  0.0 1.6 %copy-done = bf16[2,32,128,128]{3,2,1,0:T(8,128)(2,1)S(1)} copy-done((bf16[2,32,128,128]{3,2,1,0:T(8,128)(2,1)S(1)}, bf16[2,32,128,128]{3,2,1,0:T(8,128)(2,1)}, u32[]{:S(2)}) %copy-start) | copy-done | bytes 2097176
  1.6 0.0 copy-start.1
  1.6 0.7 %copy-done.1 = s32[3,1,4,128]{3,2,1,0:T(4,128)S(1)} copy-done((s32[3,1,4,128]{3,2,1,0:T(4,128)S(1)}, s32[3,1,4,128]{3,2,1,0:T(4,128)}, u32[]{:S(2)}) %copy-start.1) | copy-done | bytes 6168
  2.3 45.5 %shard_map.28 = bf16[2,16,128,128]{3,2,1,0:T(8,128)(2,1)S(1)} custom-call(bf16[2,32,128,128]{3,2,1,0:T(8,128)(2,1)S(1)} %copy-done, s32[3,1,4,128]{3,2,1,0:T(4,128)S(1)} %copy-done.1), custom_call_target="tpu_custom_call" | custom-call | tf_op jit(solution)/shard_map/pallas_call | solution.py:278
  47.8 1.0 %copy.4 = bf16[2,16,128,128]{3,2,1,0:T(8,128)(2,1)} copy(bf16[2,16,128,128]{3,2,1,0:T(8,128)(2,1)S(1)} %shard_map.28) | data formatting | bytes 2097152
Async XLA Ops:
  0.0 1.6 %copy-start = (bf16[2,32,128,128]{3,2,1,0:T(8,128)(2,1)S(1)}, bf16[2,32,128,128]{3,2,1,0:T(8,128)(2,1)}, u32[]{:S(2)}) copy-start(bf16[2,32,128,128]{3,2,1,0:T(8,128)(2,1)} %density.1) | copy-start | bytes 6291460
  1.6 0.7 %copy-start.1 = (s32[3,1,4,128]{3,2,1,0:T(4,128)S(1)}, s32[3,1,4,128]{3,2,1,0:T(4,128)}, u32[]{:S(2)}) copy-start(s32[3,1,4,128]{3,2,1,0:T(4,128)} %tasks_in.1) | copy-start | bytes 18436

commit v3 on v2

--- a/solution.py
+++ b/solution.py
@@ -275,6 +275,8 @@
         trees = 2
         chunk_bytes = slots // (trees * chunks) * size * size * density.dtype.itemsize
         own, events, tails, total = make_plan(chunks, chunk_bytes)
+        density = pltpu.with_memory_space_constraint(density, pltpu.HBM)
+        product_tasks = pltpu.with_memory_space_constraint(product_tasks, pltpu.HBM)
         return pl.pallas_call(
             functools.partial(kernel, n, own, events, tails),
             out_shape=jax.ShapeDtypeStruct((rows, mine_slots, size, size), density.dtype),

time: 48.9 us -> 46.9 us (0.959)
  local copies, waits for them, and re-layouts: 3.25 us -> 0.97 us
    unnamed x5 -> x1, local copies, waits for them, and re-layouts: 3.25 us -> 0.97 us
where the time goes in v3:
time: 46.9 us; the launch traced here: 46.7 us
  Pallas kernels  45.7 us (97%)
  local copies, waits for them, and re-layouts  0.97 us (2%)
    pallas_call x1, Pallas kernels, body(): pl.pallas_call(functools.partial(kernel, n, own, events, tails), out_shap...  45.7 us
    unnamed x1, local copies, waits for them, and re-layouts  0.97 us

profile of v3, /device:TPU:0, one launch (start us, length us, event | category | flops | bytes accessed | tf_op | source)
XLA Modules:
  0.0 46.7 jit_solution(15999689168514688281)
XLA Ops:
  0.0 45.7 %shard_map.28 = bf16[2,16,128,128]{3,2,1,0:T(8,128)(2,1)S(1)} custom-call(bf16[2,32,128,128]{3,2,1,0:T(8,128)(2,1)} %density.1, s32[3,1,4,128]{3,2,1,0:T(4,128)} %tasks_in.1), custom_call_target="tpu_custom_call" | custom-call | tf_op jit(solution)/shard_map/pallas_call | solution.py:280
  45.7 1.0 %copy.4 = bf16[2,16,128,128]{3,2,1,0:T(8,128)(2,1)} copy(bf16[2,16,128,128]{3,2,1,0:T(8,128)(2,1)S(1)} %shard_map.28) | data formatting | bytes 2097152

commit v4 on v3

--- a/solution.py
+++ b/solution.py
@@ -232,7 +232,7 @@
                     out[r, m * pair + s] = value[:, s * size : (s + 1) * size].astype(out.dtype)
                 return 0
 
-            lax.fori_loop(0, mine_slots // pair, step, 0)
+            lax.fori_loop(0, mine_slots // pair, step, 0, unroll=8)
 
     def emit_flow(spot):
         sent = len(own[spot])

time: 46.9 us -> 44.6 us (0.951)
  Pallas kernels: 45.7 us -> 43.4 us
    pallas_call x1, Pallas kernels: 45.7 us -> 43.4 us  [body(): pl.pallas_call(functools.partial(kernel, n, own, events, tails), out_shap...]
where the time goes in v4:
time: 44.6 us; the launch traced here: 44.4 us
  Pallas kernels  43.4 us (97%)
  local copies, waits for them, and re-layouts  0.97 us (2%)
    pallas_call x1, Pallas kernels, body(): pl.pallas_call(functools.partial(kernel, n, own, events, tails), out_shap...  43.4 us
    unnamed x1, local copies, waits for them, and re-layouts  0.97 us

profile of v4, /device:TPU:0, one launch (start us, length us, event | category | flops | bytes accessed | tf_op | source)
XLA Modules:
  0.0 44.4 jit_solution(10840557939545664188)
XLA Ops:
  0.0 43.4 %shard_map.28 = bf16[2,16,128,128]{3,2,1,0:T(8,128)(2,1)S(1)} custom-call(bf16[2,32,128,128]{3,2,1,0:T(8,128)(2,1)} %density.1, s32[3,1,4,128]{3,2,1,0:T(4,128)} %tasks_in.1), custom_call_target="tpu_custom_call" | custom-call | tf_op jit(solution)/shard_map/pallas_call | solution.py:280
  43.4 1.0 %copy.4 = bf16[2,16,128,128]{3,2,1,0:T(8,128)(2,1)} copy(bf16[2,16,128,128]{3,2,1,0:T(8,128)(2,1)S(1)} %shard_map.28) | data formatting | bytes 2097152
